TPU v7x, 32 devices: a whole 2x2x4 slice. The times are simulated.
32 devices in a mesh: bin: 4 (over z), row: 2 (over y), col: 4 (over x, core).
Axes of the slice: x: 2, y: 2, z: 4, core: 2. Of those that a mesh axis runs over, the one named last changes fastest.
Arguments:
- responses: bfloat16 [2, 4, 4096, 4096], P(None, 'bin', 'row', 'col'), may hold values from -6 to 6
- focusing: bfloat16 [2, 4, 16, 256, 256], P(None, 'bin', 'row'), may hold values from -0.25 to 0.25
- panel: bfloat16 [2, 4096, 256], P(None, 'col'), may hold values from -0.03125 to 0.03125
Outputs:
- projected: float32 [2, 256, 4096], P(None, 'col', 'row')
All inputs are finite; a program needn't handle non-finite values.
Results may differ from a plain program's by a relative error of at most 0.0041.
Values may be sent and summed in bfloat16 or wider, within the bound.
No kernel may reach another device: no remote copies, remote signals or barrier semaphores. Data moves between devices by JAX's collectives and lax.ppermute only.
A program may use at most 128 MiB of HBM per device.

v0:
```python
import jax
import jax.numpy as jnp
from jax import lax
from jax.sharding import PartitionSpec as P


def left_focus(blk_real, blk_imag, resp_real, resp_imag):

    def product(left_op, right_op):
        return jnp.einsum("fjab,fjbm->fjam", left_op, right_op, preferred_element_type=jnp.float32)

    return (
        product(blk_real, resp_real) - product(blk_imag, resp_imag),
        product(blk_real, resp_imag) + product(blk_imag, resp_real),
    )


def right_focus(left_real, left_imag, blk_real, blk_imag):

    def product(left_op, right_op):
        return jnp.einsum("fnjb,fjab->fnja", left_op, right_op, preferred_element_type=jnp.float32)

    return (
        product(left_real, blk_real) + product(left_imag, blk_imag),
        product(left_imag, blk_real) - product(left_real, blk_imag),
    )


def project_joint(foc_real, foc_imag, pan_real, pan_imag):

    def product(left_op, right_op):
        return jnp.einsum("fnm,mcbs->bcsn", left_op, right_op, preferred_element_type=jnp.float32)

    proj_real = product(foc_real, pan_real) - product(foc_imag, pan_imag)
    proj_imag = product(foc_real, pan_imag) + product(foc_imag, pan_real)
    return (proj_real, proj_imag)


def local(responses, focusing, panel):
    bins_here = responses.shape[1]
    tile_rows = responses.shape[2]
    tile_cols = responses.shape[3]
    row_blocks = focusing.shape[2]
    block_size = focusing.shape[3]
    col_blocks = tile_cols // block_size
    width_k = panel.shape[2]
    col_count = lax.axis_size("col")
    bin_count = lax.axis_size("bin")
    resp_real = responses[0].reshape(bins_here, row_blocks, block_size, tile_cols)
    resp_imag = responses[1].reshape(bins_here, row_blocks, block_size, tile_cols)
    left_real, left_imag = left_focus(focusing[0], focusing[1], resp_real, resp_imag)
    left_real = left_real.reshape(bins_here, tile_rows, col_blocks, block_size).astype(jnp.bfloat16)
    left_imag = left_imag.reshape(bins_here, tile_rows, col_blocks, block_size).astype(jnp.bfloat16)
    first_block = lax.axis_index("col") * col_blocks
    all_blocks = lax.all_gather(focusing, "row", axis=2, tiled=True)
    col_focus = lax.dynamic_slice_in_dim(all_blocks, first_block, col_blocks, 2)
    foc_real, foc_imag = right_focus(left_real, left_imag, col_focus[0], col_focus[1])
    foc_real = foc_real.reshape(bins_here, tile_rows, tile_cols).astype(jnp.bfloat16)
    foc_imag = foc_imag.reshape(bins_here, tile_rows, tile_cols).astype(jnp.bfloat16)
    slice_k = width_k // (col_count * bin_count)
    pan_real = panel[0].reshape(tile_cols, col_count, bin_count, slice_k)
    pan_imag = panel[1].reshape(tile_cols, col_count, bin_count, slice_k)
    proj_real, proj_imag = project_joint(foc_real, foc_imag, pan_real, pan_imag)
    partial_proj = jnp.stack(
        [proj_real.reshape(width_k, tile_rows), proj_imag.reshape(width_k, tile_rows)]
    )
    shared = lax.psum_scatter(partial_proj, ("bin", "col"), scatter_dimension=1, tiled=True)
    result = lax.all_gather(shared, "bin", axis=1, tiled=True)
    return result


def solution(mesh):
    return jax.shard_map(
        local,
        mesh=mesh,
        in_specs=(
            P(None, "bin", "row", "col"),
            P(None, "bin", "row", None, None),
            P(None, "col", None),
        ),
        out_specs=P(None, "col", "row"),
        check_vma=False,
    )
```

profile of v0, /device:TPU:0, one launch (start us, length us, event | category | flops | bytes accessed | tf_op | source)
XLA Modules:
  0.0 199.6 jit_solution(4494952446536381872)
XLA Ops:
  6.5 0.0 all-gather.3.cloned.1.call-start
  6.5 0.7 all-gather.3.cloned.1.call-update
  7.3 0.0 reduce-scatter.2.cloned.1.call-start
  7.3 0.0 copy-start.5
  7.3 4.1 %fusion.32 = (bf16[1,1,2048,1024]{3,2,1,0:T(8,128)(2,1)S(1)}, bf16[1,1,2048,1024]{3,2,1,0:T(8,128)(2,1)S(1)}) fusion(bf16[2,1,2048,1024]{3,2,1,0:T(8,128)(2,1)} %param.3), kind=kLoop, calls=%fused_computation.41 | loop fusion | bytes 16777216 | tf_op jit(solution)/shard_map/slice | solution.py:50
  11.4 0.0 copy-start
  11.4 0.0 copy-start.2
  11.4 0.0 copy-done.5
  11.4 1.3 fusion.10
  12.7 0.7 copy-done
  13.4 1.3 copy-done.2
  14.6 3.2 %subtract_convert_fusion.1 = bf16[8,256,1024]{2,1,0:T(8,128)(2,1)} fusion(f32[8,256,1024]{2,1,0:T(8,128)S(1)} %fusion.10, bf16[8,256,1024]{2,1,0:T(8,128)(2,1)S(1)} %bitcast.70, bf16[2,1,8,256,256]{4,3,2,1,0:T(8,128)(2,1)S(1)} %copy-done.5), kind=kOutput, calls=%fused_computation.3 | convolution fusion | flops 1077936128 | bytes 17825792 | tf_op jit(solution)/shard_map/fjab,fjbm->fjam/dot_general | solution.py:10
  17.9 8.2 %convert_element_type.57 = bf16[2048,4,256]{2,1,0:T(4,128)(2,1)} reshape(bf16[8,256,1024]{2,1,0:T(8,128)(2,1)} %subtract_convert_fusion.1) | data formatting | bytes 8388608 | tf_op jit(solution)/shard_map/convert_element_type | solution.py:52
  26.1 0.0 copy-start.1
  26.1 3.6 %fusion.8 = f32[8,256,1024]{2,1,0:T(8,128)S(1)} fusion(bf16[8,256,1024]{2,1,0:T(8,128)(2,1)} %bitcast.71, bf16[2,1,8,256,256]{4,3,2,1,0:T(8,128)(2,1)S(1)} %copy-done.5), kind=kOutput, calls=%fused_computation.15 | convolution fusion | flops 1073741824 | bytes 13631488 | tf_op jit(solution)/shard_map/fjab,fjbm->fjam/dot_general | solution.py:10
  29.7 0.0 copy-done.1
  29.7 3.2 %add_convert_fusion.1 = bf16[8,256,1024]{2,1,0:T(8,128)(2,1)} fusion(f32[8,256,1024]{2,1,0:T(8,128)S(1)} %fusion.8, bf16[8,256,1024]{2,1,0:T(8,128)(2,1)S(1)} %bitcast.69, bf16[2,1,8,256,256]{4,3,2,1,0:T(8,128)(2,1)S(1)} %copy-done.5), kind=kOutput, calls=%fused_computation.2 | convolution fusion | flops 1077936128 | bytes 17825792 | tf_op jit(solution)/shard_map/fjab,fjbm->fjam/dot_general | solution.py:10
  32.9 7.9 %convert_element_type.59 = bf16[2048,4,256]{2,1,0:T(4,128)(2,1)} reshape(bf16[8,256,1024]{2,1,0:T(8,128)(2,1)} %add_convert_fusion.1) | data formatting | bytes 8388608 | tf_op jit(solution)/shard_map/convert_element_type | solution.py:53
  40.7 27.6 %all-gather.3.cloned.1.call-done = bf16[2,1,16,256,256]{4,3,2,1,0:T(8,128)(2,1)} async-done(((bf16[2,1,8,256,256]{4,3,2,1,0:T(8,128)(2,1)}), bf16[2,1,16,256,256]{4,3,2,1,0:T(8,128)(2,1)}) %all-gather.3.cloned.1.call-update) | async-done | bytes 4194320 | tf_op jit(solution)/shard_map/all_gather | solution.py:55
  68.4 0.0 copy-start.3
  68.4 3.8 %fusion = f32[4,256,2048]{2,1,0:T(8,128)S(1)} fusion(bf16[2048,4,256]{2,1,0:T(4,128)(2,1)} %convert_element_type.59, bf16[2,1,16,256,256]{4,3,2,1,0:T(8,128)(2,1)} %all-gather.3.cloned.1.call-done, s32[]{:T(128)S(6)} %select_n.3), kind=kOutput, calls=%fused_computation.5 | convolution fusion | flops 1073741824 | bytes 13107204 | tf_op jit(solution)/shard_map/fnjb,fjab->fnja/dot_general | solution.py:21
  72.2 0.0 copy-done.3
  72.2 0.0 copy-start.6
  72.2 2.6 %subtract_convert_fusion = bf16[4,256,2048]{2,1,0:T(8,128)(2,1)S(1)} fusion(f32[4,256,2048]{2,1,0:T(8,128)S(1)} %fusion, bf16[2048,4,256]{2,1,0:T(4,128)(2,1)S(1)} %copy-done.3, bf16[2,1,16,256,256]{4,3,2,1,0:T(8,128)(2,1)} %all-gather.3.cloned.1.call-done, s32[]{:T(128)S(6)} %add.25, s32[]{:T(128)S(6)} %select_n.3), kind=kOutput, calls=%fused_computation | convolution fusion | flops 1077936128 | bytes 17301512 | tf_op jit(solution)/shard_map/fnjb,fjab->fnja/dot_general | solution.py:21
  74.8 0.0 copy-start.7
  74.8 0.0 copy-done.6
  74.8 1.3 fusion.18
  76.1 0.0 copy-done.7
  76.1 1.3 fusion.20
  77.4 0.0 copy-start.4
  77.4 2.5 %fusion.4 = f32[4,256,2048]{2,1,0:T(8,128)S(1)} fusion(bf16[2048,4,256]{2,1,0:T(4,128)(2,1)S(1)} %copy-done.3, bf16[2,1,16,256,256]{4,3,2,1,0:T(8,128)(2,1)} %all-gather.3.cloned.1.call-done, s32[]{:T(128)S(6)} %select_n.3), kind=kOutput, calls=%fused_computation.9 | convolution fusion | flops 1073741824 | bytes 13107204 | tf_op jit(solution)/shard_map/fnjb,fjab->fnja/dot_general | solution.py:21
  79.9 0.0 copy-done.4
  79.9 2.5 %add_convert_fusion = bf16[4,256,2048]{2,1,0:T(8,128)(2,1)S(1)} fusion(f32[4,256,2048]{2,1,0:T(8,128)S(1)} %fusion.4, bf16[2048,4,256]{2,1,0:T(4,128)(2,1)S(1)} %copy-done.4, bf16[2,1,16,256,256]{4,3,2,1,0:T(8,128)(2,1)} %all-gather.3.cloned.1.call-done, s32[]{:T(128)S(6)} %add.25, s32[]{:T(128)S(6)} %select_n.3), kind=kOutput, calls=%fused_computation.1 | convolution fusion | flops 1077936128 | bytes 17301512 | tf_op jit(solution)/shard_map/fnjb,fjab->fnja/dot_general | solution.py:21
  82.5 0.0 copy-start.8
  82.5 2.4 %fusion.22 = f32[2048,256]{0,1:S(1)} fusion(bf16[2048,1024]{0,1:T(8,128)(2,1)S(1)} %bitcast.74, bf16[2,1024,256]{2,1,0:T(8,128)(2,1)} %param.5), kind=kOutput, calls=%fused_computation.31 | convolution fusion | flops 1073741824 | bytes 6815744
  84.9 0.0 copy-done.8
  84.9 1.3 fusion.16
  86.2 0.3 add_bitcast_fusion
  86.4 0.1 copy.25
  86.6 0.3 subtract_bitcast_fusion
  86.8 0.1 copy.22
  87.0 2.2 %pad_maximum_fusion = f32[2,256,2048]{2,1,0:T(8,128)} fusion(f32[1,256,2048]{2,1,0:T(8,128)S(1)} %bitcast.72, f32[1,256,2048]{2,1,0:T(8,128)S(1)} %bitcast.73), kind=kLoop, calls=%fused_computation.4 | loop fusion | flops 1048576 | bytes 8388608 | tf_op jit(solution)/shard_map/stack | solution.py:64
  89.2 0.0 reduce-scatter.2.cloned.1.call-update
  89.3 0.0 all-gather.5.cloned.1.call-start
  89.3 72.9 %reduce-scatter.2.cloned.1.call-done = f32[2,16,2048]{2,1,0:T(8,128)} async-done(((f32[2,256,2048]{2,1,0:T(8,128)}), f32[2,16,2048]{2,1,0:T(8,128)}) %reduce-scatter.2.cloned.1.call-update) | async-done | bytes 262160 | tf_op jit(solution)/shard_map/reduce_scatter | solution.py:67
  162.2 0.0 all-gather.5.cloned.1.call-update
  162.2 28.6 %all-gather.5.cloned.1.call-done = f32[2,64,2048]{2,1,0:T(8,128)} async-done(((f32[2,16,2048]{2,1,0:T(8,128)}), f32[2,64,2048]{2,1,0:T(8,128)}) %all-gather.5.cloned.1.call-update) | async-done | bytes 1048592 | tf_op jit(solution)/shard_map/all_gather | solution.py:68
  190.8 2.3 %copy.39 = f32[2,64,2048]{2,1,0:T(8,128)} copy(f32[2,64,2048]{2,1,0:T(8,128)} %all-gather.5.cloned.1.call-done) | data formatting | bytes 2097152
Async XLA Ops:
  6.5 61.8 %all-gather.3.cloned.1.call-start = ((), (), s32[]{:S(2)}) async-start(), calls=%async_computation.1 | async-start | bytes 6291456 | tf_op jit(solution)/shard_map/all_gather | solution.py:55
  7.3 154.9 %reduce-scatter.2.cloned.1.call-start = ((), (), s32[]{:S(2)}) async-start(), calls=%async_computation.2 | async-start | bytes 4456448 | tf_op jit(solution)/shard_map/reduce_scatter | solution.py:67
  7.3 4.1 %copy-start.5 = (bf16[2,1,8,256,256]{4,3,2,1,0:T(8,128)(2,1)S(1)}, bf16[2,1,8,256,256]{4,3,2,1,0:T(8,128)(2,1)}, u32[]{:S(2)}) copy-start(bf16[2,1,8,256,256]{4,3,2,1,0:T(8,128)(2,1)} %param.4) | copy-start | bytes 6291460
  11.4 2.0 copy-start
  11.4 3.2 %copy-start.2 = (bf16[1,1,2048,1024]{3,2,1,0:T(8,128)(2,1)}, bf16[1,1,2048,1024]{3,2,1,0:T(8,128)(2,1)S(1)}, u32[]{:S(2)}) copy-start(bf16[1,1,2048,1024]{3,2,1,0:T(8,128)(2,1)S(1)} %get-tuple-element.5) | copy-start | bytes 12582916
  26.1 3.6 %copy-start.1 = (bf16[1,1,2048,1024]{3,2,1,0:T(8,128)(2,1)S(1)}, bf16[1,1,2048,1024]{3,2,1,0:T(8,128)(2,1)}, u32[]{:S(2)}) copy-start(bf16[1,1,2048,1024]{3,2,1,0:T(8,128)(2,1)} %copy-done) | copy-start | bytes 12582916
  68.4 3.8 %copy-start.3 = (bf16[2048,4,256]{2,1,0:T(4,128)(2,1)S(1)}, bf16[2048,4,256]{2,1,0:T(4,128)(2,1)}, u32[]{:S(2)}) copy-start(bf16[2048,4,256]{2,1,0:T(4,128)(2,1)} %convert_element_type.57) | copy-start | bytes 12582916
  72.2 2.6 %copy-start.6 = (bf16[2,1024,256]{2,1,0:T(8,128)(2,1)S(1)}, bf16[2,1024,256]{2,1,0:T(8,128)(2,1)}, u32[]{:S(2)}) copy-start(bf16[2,1024,256]{2,1,0:T(8,128)(2,1)} %param.5) | copy-start | bytes 3145732
  74.8 1.3 copy-start.7
  77.4 2.5 %copy-start.4 = (bf16[2048,4,256]{2,1,0:T(4,128)(2,1)S(1)}, bf16[2048,4,256]{2,1,0:T(4,128)(2,1)}, u32[]{:S(2)}) copy-start(bf16[2048,4,256]{2,1,0:T(4,128)(2,1)} %convert_element_type.59) | copy-start | bytes 12582916
  82.5 2.4 %copy-start.8 = (bf16[2,1024,256]{2,1,0:T(8,128)(2,1)S(1)}, bf16[2,1024,256]{2,1,0:T(8,128)(2,1)}, u32[]{:S(2)}) copy-start(bf16[2,1024,256]{2,1,0:T(8,128)(2,1)} %param.5) | copy-start | bytes 3145732
  89.3 101.6 %all-gather.5.cloned.1.call-start = ((), (), s32[]{:S(2)}) async-start(), calls=%async_computation.3 | async-start | bytes 1310720 | tf_op jit(solution)/shard_map/all_gather | solution.py:68
Sparse Core Ops, SparseCore 0:
  8.9 59.4 all-gather.2
  89.4 72.7 reduce-scatter.1
  163.8 27.0 all-gather.4
where the time goes:
time: 200 us
  waiting for transfers between devices  130 us (65%)
  matrix products  29 us (14%)
  local copies, waits for them, and re-layouts  24.7 us (12%)
  between operations  13.3 us (7%)
  other arithmetic  2.74 us (1%)
    reduce_scatter x1, waiting for transfers between devices, local(): lax.psum_scatter(partial_proj, ('bin', 'col'), scatter_dimension=1, tiled...  72.9 us
    all_gather x1, waiting for transfers between devices, local(): result = lax.all_gather(shared, 'bin', axis=1, tiled=True)  28.6 us
    all_gather x1, waiting for transfers between devices, local(): all_blocks = lax.all_gather(focusing, 'row', axis=2, tiled=True)  27.6 us
    dot_general x4, matrix products, product(): jnp.einsum('fnjb,fjab->fnja', left_op, right_op, preferred_element_type=j...  11.5 us
    dot_general x4, matrix products, product(): jnp.einsum('fjab,fjbm->fjam', left_op, right_op, preferred_element_type=j...  11.3 us
    convert_element_type x1, local copies, waits for them, and re-layouts, local(): left_real.reshape(bins_here, tile_rows, col_blocks, block_size)  8.18 us
    convert_element_type x1, local copies, waits for them, and re-layouts, local(): left_imag.reshape(bins_here, tile_rows, col_blocks, block_size)  7.88 us
    unnamed x4, matrix products  6.21 us
  transfers between devices with their start and end apart: 3, of which 3 were waited for; matrix products, arithmetic and copies ran while one was open for 16% of the time, Pallas kernels for 0%

commit v1 on v0

--- a/solution.py
+++ b/solution.py
@@ -52,7 +52,14 @@
     left_real = left_real.reshape(bins_here, tile_rows, col_blocks, block_size).astype(jnp.bfloat16)
     left_imag = left_imag.reshape(bins_here, tile_rows, col_blocks, block_size).astype(jnp.bfloat16)
     first_block = lax.axis_index("col") * col_blocks
-    all_blocks = lax.all_gather(focusing, "row", axis=2, tiled=True)
+    ways, here, lap = (lax.axis_size("row"), lax.axis_index("row"), focusing.shape[2])
+    line, have = (focusing, 1)
+    while have < ways:
+        line = jnp.concatenate(
+            [line, lax.ppermute(line, "row", [(d, (d - have) % ways) for d in range(ways)])], axis=2
+        )
+        have = 2 * have
+    all_blocks = jnp.roll(line, here * lap, axis=2)
     col_focus = lax.dynamic_slice_in_dim(all_blocks, first_block, col_blocks, 2)
     foc_real, foc_imag = right_focus(left_real, left_imag, col_focus[0], col_focus[1])
     foc_real = foc_real.reshape(bins_here, tile_rows, tile_cols).astype(jnp.bfloat16)

time: 200 us -> 191 us (0.955)
  waiting for transfers between devices: 130 us -> 109 us
  matrix products: 29 us -> 36.7 us
  starting transfers between devices: 0.08 us -> 3.04 us
    all_gather x1 -> x0, waiting for transfers between devices: 27.6 us -> none  [local(): all_blocks = lax.all_gather(focusing, 'row', axis=2, tiled=True)]
    dot_general x4, matrix products: 11.3 us -> 19.2 us  [product(): jnp.einsum('fjab,fjbm->fjam', left_op, right_op, preferred_element_type=j...]
    ppermute x0 -> x1, waiting for transfers between devices: none -> 5.86 us  [local(): lax.ppermute(line, 'row', [(d, (d - have) % ways) for d in range(ways)])]
    dot_general x4, matrix products: 11.5 us -> 7.51 us  [product(): jnp.einsum('fnjb,fjab->fnja', left_op, right_op, preferred_element_type=j...]
    unnamed x4, matrix products: 6.21 us -> 10 us
    ppermute x0 -> x1, starting transfers between devices: none -> 3 us  [local(): lax.ppermute(line, 'row', [(d, (d - have) % ways) for d in range(ways)])]
  transfers between devices with their start and end apart: 3 -> 3, of which waited for: 3 -> 3; matrix products, arithmetic and copies ran while one was open for 16% -> 21% of each run, Pallas kernels for 0% -> 0%
where the time goes in v1:
time: 191 us
  waiting for transfers between devices  109 us (57%)
  matrix products  36.7 us (19%)
  local copies, waits for them, and re-layouts  24.9 us (13%)
  between operations  13.5 us (7%)
  other arithmetic  3.51 us (2%)
  starting transfers between devices  3.04 us (2%)
    reduce_scatter x1, waiting for transfers between devices, local(): lax.psum_scatter(partial_proj, ('bin', 'col'), scatter_dimension=1, tiled...  74.6 us
    all_gather x1, waiting for transfers between devices, local(): result = lax.all_gather(shared, 'bin', axis=1, tiled=True)  28.6 us
    dot_general x4, matrix products, product(): jnp.einsum('fjab,fjbm->fjam', left_op, right_op, preferred_element_type=j...  19.2 us
    unnamed x4, matrix products  10 us
    convert_element_type x1, local copies, waits for them, and re-layouts, local(): left_real.reshape(bins_here, tile_rows, col_blocks, block_size)  7.87 us
    convert_element_type x1, local copies, waits for them, and re-layouts, local(): left_imag.reshape(bins_here, tile_rows, col_blocks, block_size)  7.82 us
    dot_general x4, matrix products, product(): jnp.einsum('fnjb,fjab->fnja', left_op, right_op, preferred_element_type=j...  7.51 us
    ppermute x1, waiting for transfers between devices, local(): lax.ppermute(line, 'row', [(d, (d - have) % ways) for d in range(ways)])  5.86 us
  transfers between devices with their start and end apart: 3, of which 3 were waited for; matrix products, arithmetic and copies ran while one was open for 21% of the time, Pallas kernels for 0%

profile of v1, /device:TPU:0, one launch (start us, length us, event | category | flops | bytes accessed | tf_op | source)
XLA Modules:
  0.0 190.7 jit_solution(13497556214604273211)
XLA Ops:
  6.5 0.0 copy-start.4
  6.5 0.0 reduce-scatter.2.cloned.1.call-start
  6.5 3.0 %collective-permute-start = (bf16[2,1,8,256,256]{4,3,2,1,0:T(8,128)(2,1)}, bf16[2,1,8,256,256]{4,3,2,1,0:T(8,128)(2,1)}, u32[]{:S(2)}, u32[]{:S(2)}) collective-permute-start(bf16[2,1,8,256,256]{4,3,2,1,0:T(8,128)(2,1)} %param.4), channel_id=1, source_target_pairs={{0,4},{4,0},{1,5},{5,1},{2,6},{6,2},{3,7},{7,3},{8,12},{12,8},{9,1... | collective-permute-start | bytes 6291464 | tf_op jit(solution)/shard_map/ppermute | solution.py:59
  9.5 5.2 %fusion.31 = (bf16[1,1,2048,1024]{3,2,1,0:T(8,128)(2,1)}, bf16[1,1,2048,1024]{3,2,1,0:T(8,128)(2,1)S(1)}) fusion(bf16[2,1,2048,1024]{3,2,1,0:T(8,128)(2,1)} %param.3), kind=kLoop, calls=%fused_computation.44 | loop fusion | bytes 16777216 | tf_op jit(solution)/shard_map/slice | solution.py:49
  14.8 0.0 copy-start
  14.8 0.0 copy-done.4
  14.8 4.5 %fusion.11 = f32[8,256,1024]{2,1,0:T(8,128)} fusion(bf16[8,256,1024]{2,1,0:T(8,128)(2,1)S(1)} %bitcast.68, bf16[2,1,8,256,256]{4,3,2,1,0:T(8,128)(2,1)S(1)} %copy-done.4), kind=kOutput, calls=%fused_computation.22 | convolution fusion | flops 1073741824 | bytes 13631488 | tf_op jit(solution)/shard_map/fjab,fjbm->fjam/dot_general | solution.py:10
  19.3 0.0 copy-done
  19.3 7.9 %add_convert_fusion.1 = bf16[8,256,1024]{2,1,0:T(8,128)(2,1)} fusion(f32[8,256,1024]{2,1,0:T(8,128)} %fusion.11, bf16[8,256,1024]{2,1,0:T(8,128)(2,1)} %bitcast.70, bf16[2,1,8,256,256]{4,3,2,1,0:T(8,128)(2,1)S(1)} %copy-done.4), kind=kOutput, calls=%fused_computation.6 | convolution fusion | flops 1077936128 | bytes 17825792 | tf_op jit(solution)/shard_map/fjab,fjbm->fjam/dot_general | solution.py:10
  27.1 7.8 %convert_element_type.59 = bf16[2048,4,256]{2,1,0:T(4,128)(2,1)} reshape(bf16[8,256,1024]{2,1,0:T(8,128)(2,1)} %add_convert_fusion.1) | data formatting | bytes 8388608 | tf_op jit(solution)/shard_map/convert_element_type | solution.py:53
  35.0 0.0 copy-start.1
  35.0 3.6 %fusion.13 = f32[8,256,1024]{2,1,0:T(8,128)S(1)} fusion(bf16[8,256,1024]{2,1,0:T(8,128)(2,1)} %bitcast.71, bf16[2,1,8,256,256]{4,3,2,1,0:T(8,128)(2,1)S(1)} %copy-done.4), kind=kOutput, calls=%fused_computation.24 | convolution fusion | flops 1073741824 | bytes 13631488 | tf_op jit(solution)/shard_map/fjab,fjbm->fjam/dot_general | solution.py:10
  38.6 0.0 copy-done.1
  38.6 3.2 %subtract_convert_fusion.1 = bf16[8,256,1024]{2,1,0:T(8,128)(2,1)} fusion(f32[8,256,1024]{2,1,0:T(8,128)S(1)} %fusion.13, bf16[8,256,1024]{2,1,0:T(8,128)(2,1)S(1)} %bitcast.69, bf16[2,1,8,256,256]{4,3,2,1,0:T(8,128)(2,1)S(1)} %copy-done.4), kind=kOutput, calls=%fused_computation.7 | convolution fusion | flops 1077936128 | bytes 17825792 | tf_op jit(solution)/shard_map/fjab,fjbm->fjam/dot_general | solution.py:10
  41.8 7.9 %convert_element_type.57 = bf16[2048,4,256]{2,1,0:T(4,128)(2,1)} reshape(bf16[8,256,1024]{2,1,0:T(8,128)(2,1)} %subtract_convert_fusion.1) | data formatting | bytes 8388608 | tf_op jit(solution)/shard_map/convert_element_type | solution.py:52
  49.7 0.0 copy-start.3
  49.7 5.9 %collective-permute-done = bf16[2,1,8,256,256]{4,3,2,1,0:T(8,128)(2,1)} collective-permute-done((bf16[2,1,8,256,256]{4,3,2,1,0:T(8,128)(2,1)}, bf16[2,1,8,256,256]{4,3,2,1,0:T(8,128)(2,1)}, u32[]{:S(2)}, u32[]{:S(2)}) %collective-permute-start) | collective-permute-done | bytes 2097184 | tf_op jit(solution)/shard_map/ppermute | solution.py:59
  55.5 0.8 fusion.8
  56.3 0.0 copy-done.3
  56.3 0.0 copy-start.2
  56.4 1.3 fusion.3
  57.7 0.9 copy-done.2
  58.5 3.4 %subtract_convert_fusion = bf16[4,256,2048]{2,1,0:T(8,128)(2,1)} fusion(f32[4,256,2048]{2,1,0:T(8,128)S(1)} %fusion.3, bf16[2048,4,256]{2,1,0:T(4,128)(2,1)S(1)} %copy-done.2, bf16[2,1,4,256,256]{4,3,2,1,0:T(8,128)(2,1)S(1)} %fusion.8), kind=kOutput, calls=%fused_computation.4 | convolution fusion | flops 1077936128 | bytes 17301504 | tf_op jit(solution)/shard_map/fnjb,fjab->fnja/dot_general | solution.py:21
  62.0 0.0 copy-start.5
  62.0 0.0 copy-start.7
  62.0 3.8 %fusion.21 = f32[2048,256]{0,1:S(1)} fusion(bf16[2048,1024]{0,1:T(8,128)(2,1)} %bitcast.76, bf16[2,1024,256]{2,1,0:T(8,128)(2,1)} %param.5), kind=kOutput, calls=%fused_computation.34 | convolution fusion | flops 1073741824 | bytes 6815744
  65.7 0.0 copy-done.5
  65.7 0.1 copy-done.7
  65.9 2.6 %fusion.23 = f32[2048,256]{0,1} fusion(bf16[2048,1024]{0,1:T(8,128)(2,1)S(1)} %bitcast.77, bf16[2,1024,256]{2,1,0:T(8,128)(2,1)S(1)} %copy-done.7), kind=kOutput, calls=%fused_computation.36 | convolution fusion | flops 1073741824 | bytes 6815744
  68.5 1.3 fusion.1
  69.8 1.5 add_convert_fusion
  71.3 0.0 copy-start.8
  71.3 2.4 %fusion.25 = f32[2048,256]{0,1:S(1)} fusion(bf16[2048,1024]{0,1:T(8,128)(2,1)S(1)} %bitcast.74, bf16[2,1024,256]{2,1,0:T(8,128)(2,1)} %param.5), kind=kOutput, calls=%fused_computation.38 | convolution fusion | flops 1073741824 | bytes 6815744
  73.7 0.0 copy-done.8
  73.7 0.0 copy-start.6
  73.7 1.3 fusion.19
  75.0 0.3 copy-done.6
  75.3 0.2 add_bitcast_fusion
  75.6 0.1 copy.25
  75.7 0.3 subtract_bitcast_fusion
  76.0 0.1 copy.22
  76.1 2.2 %pad_maximum_fusion = f32[2,256,2048]{2,1,0:T(8,128)} fusion(f32[1,256,2048]{2,1,0:T(8,128)S(1)} %bitcast.72, f32[1,256,2048]{2,1,0:T(8,128)S(1)} %bitcast.73), kind=kLoop, calls=%fused_computation.8 | loop fusion | flops 1048576 | bytes 8388608 | tf_op jit(solution)/shard_map/stack | solution.py:71
  78.3 0.0 reduce-scatter.2.cloned.1.call-update
  78.4 0.0 all-gather.2.cloned.1.call-start
  78.4 74.6 %reduce-scatter.2.cloned.1.call-done = f32[2,16,2048]{2,1,0:T(8,128)} async-done(((f32[2,256,2048]{2,1,0:T(8,128)}), f32[2,16,2048]{2,1,0:T(8,128)}) %reduce-scatter.2.cloned.1.call-update) | async-done | bytes 262160 | tf_op jit(solution)/shard_map/reduce_scatter | solution.py:74
  153.0 0.0 all-gather.2.cloned.1.call-update
  153.0 28.6 %all-gather.2.cloned.1.call-done = f32[2,64,2048]{2,1,0:T(8,128)} async-done(((f32[2,16,2048]{2,1,0:T(8,128)}), f32[2,64,2048]{2,1,0:T(8,128)}) %all-gather.2.cloned.1.call-update) | async-done | bytes 1048592 | tf_op jit(solution)/shard_map/all_gather | solution.py:75
  181.6 2.3 %copy.39 = f32[2,64,2048]{2,1,0:T(8,128)} copy(f32[2,64,2048]{2,1,0:T(8,128)} %all-gather.2.cloned.1.call-done) | data formatting | bytes 2097152
Async XLA Ops:
  6.5 8.2 %copy-start.4 = (bf16[2,1,8,256,256]{4,3,2,1,0:T(8,128)(2,1)S(1)}, bf16[2,1,8,256,256]{4,3,2,1,0:T(8,128)(2,1)}, u32[]{:S(2)}) copy-start(bf16[2,1,8,256,256]{4,3,2,1,0:T(8,128)(2,1)} %param.4) | copy-start | bytes 6291460
  6.5 146.5 %reduce-scatter.2.cloned.1.call-start = ((), (), s32[]{:S(2)}) async-start(), calls=%async_computation.1 | async-start | bytes 4456448 | tf_op jit(solution)/shard_map/reduce_scatter | solution.py:74
  6.5 49.0 %collective-permute-start = (bf16[2,1,8,256,256]{4,3,2,1,0:T(8,128)(2,1)}, bf16[2,1,8,256,256]{4,3,2,1,0:T(8,128)(2,1)}, u32[]{:S(2)}, u32[]{:S(2)}) collective-permute-start(bf16[2,1,8,256,256]{4,3,2,1,0:T(8,128)(2,1)} %param.4), channel_id=1, source_target_pairs={{0,4},{4,0},{1,5},{5,1},{2,6},{6,2},{3,7},{7,3},{8,12},{12,8},{9,1... | collective-permute-start | bytes 6291464 | tf_op jit(solution)/shard_map/ppermute | solution.py:59
  14.8 4.5 %copy-start = (bf16[1,1,2048,1024]{3,2,1,0:T(8,128)(2,1)}, bf16[1,1,2048,1024]{3,2,1,0:T(8,128)(2,1)S(1)}, u32[]{:S(2)}) copy-start(bf16[1,1,2048,1024]{3,2,1,0:T(8,128)(2,1)S(1)} %get-tuple-element.6) | copy-start | bytes 12582916
  35.0 3.6 %copy-start.1 = (bf16[1,1,2048,1024]{3,2,1,0:T(8,128)(2,1)S(1)}, bf16[1,1,2048,1024]{3,2,1,0:T(8,128)(2,1)}, u32[]{:S(2)}) copy-start(bf16[1,1,2048,1024]{3,2,1,0:T(8,128)(2,1)} %copy-done) | copy-start | bytes 12582916
  49.7 6.7 %copy-start.3 = (bf16[2048,4,256]{2,1,0:T(4,128)(2,1)S(1)}, bf16[2048,4,256]{2,1,0:T(4,128)(2,1)}, u32[]{:S(2)}) copy-start(bf16[2048,4,256]{2,1,0:T(4,128)(2,1)} %convert_element_type.57) | copy-start | bytes 12582916
  56.3 2.2 %copy-start.2 = (bf16[2048,4,256]{2,1,0:T(4,128)(2,1)S(1)}, bf16[2048,4,256]{2,1,0:T(4,128)(2,1)}, u32[]{:S(2)}) copy-start(bf16[2048,4,256]{2,1,0:T(4,128)(2,1)} %convert_element_type.59) | copy-start | bytes 12582916
  62.0 3.8 %copy-start.5 = (bf16[4,256,2048]{2,1,0:T(8,128)(2,1)S(1)}, bf16[4,256,2048]{2,1,0:T(8,128)(2,1)}, u32[]{:S(2)}) copy-start(bf16[4,256,2048]{2,1,0:T(8,128)(2,1)} %subtract_convert_fusion) | copy-start | bytes 12582916
  62.0 3.9 %copy-start.7 = (bf16[2,1024,256]{2,1,0:T(8,128)(2,1)S(1)}, bf16[2,1024,256]{2,1,0:T(8,128)(2,1)}, u32[]{:S(2)}) copy-start(bf16[2,1024,256]{2,1,0:T(8,128)(2,1)} %param.5) | copy-start | bytes 3145732
  71.3 2.4 %copy-start.8 = (bf16[2,1024,256]{2,1,0:T(8,128)(2,1)S(1)}, bf16[2,1024,256]{2,1,0:T(8,128)(2,1)}, u32[]{:S(2)}) copy-start(bf16[2,1024,256]{2,1,0:T(8,128)(2,1)} %param.5) | copy-start | bytes 3145732
  73.7 1.6 copy-start.6
  78.4 103.2 %all-gather.2.cloned.1.call-start = ((), (), s32[]{:S(2)}) async-start(), calls=%async_computation.2 | async-start | bytes 1310720 | tf_op jit(solution)/shard_map/all_gather | solution.py:75
Sparse Core Ops, SparseCore 0:
  78.5 74.4 reduce-scatter.1
  154.6 26.9 all-gather.1
